TPU v7x, 32 devices: a whole 2x2x4 slice. The times are simulated.
32 devices in a mesh: tile: 8 (over z, x), grp: 4 (over y, core).
Axes of the slice: x: 2, y: 2, z: 4, core: 2. Of those that a mesh axis runs over, the one named last changes fastest.
Arguments:
- pixels: bfloat16 [8192, 432], P(('tile', 'grp')), may hold values from -25 to 25
- labels: int32 [8192], P(('tile', 'grp')), may hold values from 0 to 63, as said below
- targets: bfloat16 [512, 432], P('grp'), may hold values from -6 to 6
Outputs:
- scores: bfloat16 [8192, 512], P(('tile', 'grp'))
Inputs may be any that keep to these rules, and one draw needn't show every extreme that they name: `labels`: among the 256 pixels of each aligned block (rows b * 256 to (b + 1) * 256 - 1) no cluster occurs more than 8 times; in every draw one cluster occurs exactly 8 times in every block.
All inputs are finite; a program needn't handle non-finite values.
Results may differ from a plain program's by a relative error of at most 0.0024.
Values may be sent and summed in bfloat16 or wider, within the bound.
A program may use at most 128 MiB of HBM per device.

v0:
```python
import functools

import jax
import jax.numpy as jnp
from jax import lax
from jax.experimental import pallas as pl
from jax.experimental.pallas import tpu as pltpu
from jax.sharding import PartitionSpec as P

NCLUST = 64
CAP = 8
RIDGE = 0.05
LIFT = 1.0
EPS = 1e-06
STEP = 64
LANES = 128
SUB = 8
PIV = 4
MESH = pl.DeviceIdType.MESH
HI = lax.Precision.HIGHEST
F32 = jnp.float32
BF16 = jnp.bfloat16


def dot_t(a, b, prec=None):
    return lax.dot_general(a, b, (((1,), (1,)), ((), ())), precision=prec, preferred_element_type=F32)


def dot_0(a, b, prec=None):
    return lax.dot_general(a, b, (((0,), (0,)), ((), ())), precision=prec, preferred_element_type=F32)


def dot_n(a, b, prec=None):
    return lax.dot_general(a, b, (((1,), (0,)), ((), ())), precision=prec, preferred_element_type=F32)


def halves(v):
    big = v.astype(BF16)
    return big, (v - big.astype(F32)).astype(BF16)


def thirds(v):
    big, rest = v.astype(BF16), v
    rest = rest - big.astype(F32)
    mid = rest.astype(BF16)
    return big, mid, (rest - mid.astype(F32)).astype(BF16)


def outer_update(a, b):
    a1, a2, a3 = thirds(a)
    b1, b2, b3 = thirds(b)
    left = jnp.concatenate([a1, a1, a2, a1, a2, a3], axis=0)
    right = jnp.concatenate([b1, b2, b1, b3, b2, b1], axis=0)
    return dot_0(left, right)


def pivot_inverse(e):
    r = 1.0 / (e[0][0] * e[1][1] - e[0][1] * e[0][1])
    i00, i01, i11 = e[1][1] * r, -e[0][1] * r, e[0][0] * r
    x00 = i00 * e[0][2] + i01 * e[1][2]
    x01 = i00 * e[0][3] + i01 * e[1][3]
    x10 = i01 * e[0][2] + i11 * e[1][2]
    x11 = i01 * e[0][3] + i11 * e[1][3]
    s00 = e[2][2] - (e[0][2] * x00 + e[1][2] * x10)
    s01 = e[2][3] - (e[0][2] * x01 + e[1][2] * x11)
    s11 = e[3][3] - (e[0][3] * x01 + e[1][3] * x11)
    q = 1.0 / (s00 * s11 - s01 * s01)
    t00, t01, t11 = s11 * q, -s01 * q, s00 * q
    y00 = -(x00 * t00 + x01 * t01)
    y01 = -(x00 * t01 + x01 * t11)
    y10 = -(x10 * t00 + x11 * t01)
    y11 = -(x10 * t01 + x11 * t11)
    n00 = i00 - (y00 * x00 + y01 * x01)
    n01 = i01 - (y00 * x10 + y01 * x11)
    n11 = i11 - (y10 * x10 + y11 * x11)
    return [[n00, n01, y00, y01], [n01, n11, y10, y11], [y00, y10, t00, t01], [y01, y11, t01, t11]]


def panel_step(tiles, first, j):
    rows = tiles[0].shape[0]
    at = first + j
    home, off = at // LANES, at % LANES
    group = j // SUB * SUB
    lane8 = lax.broadcasted_iota(jnp.int32, (SUB, LANES), 1)
    lanes = lax.broadcasted_iota(jnp.int32, (rows, LANES), 1)
    sub8 = lax.broadcasted_iota(jnp.int32, (SUB, LANES), 0)
    cols = [jnp.broadcast_to(tiles[home][:, off + c : off + c + 1], (rows, LANES)) for c in range(PIV)]
    spread = lambda v, a: jnp.broadcast_to(v[j + a : j + a + 1, :], (SUB, LANES))
    inv = pivot_inverse([[spread(cols[c], a) for c in range(PIV)] for a in range(PIV)])
    fresh = []
    for t, tile in enumerate(tiles):
        src = [spread(tile, c) for c in range(PIV)]
        kept = tile
        if t == home:
            block = (lane8 >= off) & (lane8 < off + PIV)
            src = [jnp.where(block, jnp.where(lane8 == off + c, 1.0, 0.0), v) for c, v in enumerate(src)]
            kept = jnp.where((lanes >= off) & (lanes < off + PIV), 0.0, tile)
        norm = [(inv[a][0] * src[0] + inv[a][1] * src[1]) + (inv[a][2] * src[2] + inv[a][3] * src[3]) for a in range(PIV)]
        wide = [jnp.concatenate([v] * (rows // SUB), axis=0) for v in norm]
        rest = kept - ((cols[0] * wide[0] + cols[1] * wide[1]) + (cols[2] * wide[2] + cols[3] * wide[3]))
        own = rest[group : group + SUB]
        for a in range(PIV):
            own = jnp.where(sub8 == j - group + a, norm[a], own)
        parts = [rest[:group]] * (group > 0) + [own] + [rest[group + SUB :]] * (group + SUB < rows)
        fresh.append(jnp.concatenate(parts, axis=0) if len(parts) > 1 else parts[0])
    return fresh


def panel_inverse(panels, first):
    rows, width = panels[0].shape
    split = [[p[:, t : t + LANES] for t in range(0, width, LANES)] for p in panels]
    for j in range(0, rows, PIV):
        split = [panel_step(tiles, first, j) for tiles in split]
    return [jnp.concatenate(tiles, axis=1) for tiles in split]


def invert_all(mats, midway):
    size = mats[0].shape[0]
    lane1 = lax.broadcasted_iota(jnp.int32, (1, size), 1)
    for k in range(size // STEP):
        lo = k * STEP
        if k == size // STEP // 2:
            midway()
        inside = (lane1 >= lo) & (lane1 < lo + STEP)
        sign = jnp.where(lane1 < lo, -1.0, jnp.where(inside, 0.0, 1.0))
        rows = [m[lo : lo + STEP, :] for m in mats]
        outs = panel_inverse(rows, lo)
        fresh = []
        for m, r, w in zip(mats, rows, outs):
            kept = jnp.where(inside, 0.0, m)
            upd = kept - outer_update(r * sign, w)
            parts = [upd[:lo]] * (lo > 0) + [w] + [upd[lo + STEP :]] * (lo + STEP < size)
            fresh.append(jnp.concatenate(parts, axis=0))
        mats = fresh
    return mats


def cluster_gram(x, bands):
    size = x.shape[0]
    gram = dot_t(x, x)
    valid = x[:, bands : bands + 1].astype(F32)
    ri = lax.broadcasted_iota(jnp.int32, (size, size), 0)
    ci = lax.broadcasted_iota(jnp.int32, (size, size), 1)
    diag = ri == ci
    valid_row = jnp.sum(jnp.where(diag, valid, 0.0), axis=0, keepdims=True)
    count = jnp.maximum(jnp.sum(valid), 1.0)
    share = 1.0 / count
    mean_r = jnp.sum(gram, axis=0, keepdims=True) * share
    mean_c = jnp.sum(gram, axis=1, keepdims=True) * share
    mean = jnp.sum(mean_r) * share
    mat = (gram - mean_r - mean_c + (mean + LIFT)) * (valid * valid_row) * share
    mat = mat + jnp.where(diag, RIDGE, 0.0)
    return mat, valid, count, diag


def cluster_scores(u, tnorm, inverse, count, diag, bands):
    share = 1.0 / count
    (k1, k2), (u1, u2) = halves(inverse), halves(u)
    z = dot_n(k1, u1) + (dot_n(k1, u2) + dot_n(k2, u1))
    kd = jnp.sum(jnp.where(diag, inverse, 0.0), axis=1, keepdims=True)
    pix = count * (1.0 - RIDGE * kd) - LIFT / (LIFT + RIDGE)
    pix = jnp.maximum(pix, 0.0) + EPS
    lib = (tnorm - jnp.sum(u * z, axis=0, keepdims=True) * share) * (1.0 / RIDGE)
    lib = jnp.maximum(lib, 0.0) + EPS
    return z * z * (bands / pix) * (1.0 / lib)


def slot_of(lab_row, slots):
    count = lab_row.shape[1]
    ri = lax.broadcasted_iota(jnp.int32, (count, count), 0)
    ci = lax.broadcasted_iota(jnp.int32, (count, count), 1)
    lab_row = lab_row.astype(F32)
    lab_col = jnp.sum(jnp.where(ri == ci, lab_row, 0.0), axis=1, keepdims=True)
    same = jnp.where(lab_row == lab_col, 1.0, 0.0)
    rank_col = jnp.sum(jnp.where(ci < ri, same, 0.0), axis=1, keepdims=True)
    rank_row = jnp.sum(jnp.where(ri < ci, same, 0.0), axis=0, keepdims=True)
    idx_col = lab_col * CAP + rank_col
    idx_row = lab_row * CAP + rank_row
    across = lax.broadcasted_iota(jnp.int32, (count, slots), 1).astype(F32)
    down = lax.broadcasted_iota(jnp.int32, (slots, count), 0).astype(F32)
    take = jnp.where(across == idx_col, 1.0, 0.0).astype(BF16)
    put = jnp.where(down == idx_row, 1.0, 0.0).astype(BF16)
    return take, put


def step_body(
    bands, owned, n_tile, n_grp,
    lab_ref, pix_ref, tgt_ref, out_ref,
    wide, outgoing, arrived, mine, library, outbound, returned, take_ref,
    send_a, recv_a, send_t, recv_t, send_b, recv_b,
):
    devices = n_tile * n_grp
    group = owned * CAP
    slots = devices * group
    width = wide.shape[1]
    total = outbound.shape[2]
    tile = lax.axis_index("tile")
    grp = lax.axis_index("grp")
    me = tile * n_grp + grp

    def place(r):
        other = lax.rem(me + r, devices)
        return (lax.div(other, n_grp), lax.rem(other, n_grp)), other

    barrier = pltpu.get_barrier_semaphore()

    def greet(r, _):
        pl.semaphore_signal(barrier, inc=1, device_id=place(r)[0], device_id_type=MESH)
        return 0

    lax.fori_loop(1, devices, greet, 0)

    wide[...] = jnp.ones_like(wide)
    wide[:, :bands] = pix_ref[...]
    mine[...] = jnp.zeros_like(mine)
    mine[:, :bands] = tgt_ref[...]
    take, put = slot_of(lab_ref[...], slots)
    take_ref[...] = take
    outgoing[...] = dot_n(put, wide[...]).astype(BF16).reshape(devices, group, width)
    pl.semaphore_wait(barrier, devices - 1)

    def ship(src, dst, sends, recvs, r):
        where, other = place(r)
        return pltpu.make_async_remote_copy(
            src_ref=src.at[other], dst_ref=dst.at[me],
            send_sem=sends.at[r], recv_sem=recvs.at[r],
            device_id=where, device_id_type=MESH,
        )

    def lend(r):
        return pltpu.make_async_remote_copy(
            src_ref=mine, dst_ref=library.at[grp],
            send_sem=send_t.at[r], recv_sem=recv_t.at[r],
            device_id=(tile, lax.rem(grp + r, n_grp)), device_id_type=MESH,
        )

    def start_a(r, _):
        ship(outgoing, arrived, send_a, recv_a, r).start()
        return 0

    def wait_a(r, _):
        ship(outgoing, arrived, send_a, recv_a, r).wait()
        return 0

    def start_b(r, _):
        ship(outbound, returned, send_b, recv_b, r).start()
        return 0

    def wait_b(r, _):
        ship(outbound, returned, send_b, recv_b, r).wait()
        return 0

    lax.fori_loop(1, devices, start_a, 0)
    for r in range(1, n_grp):
        lend(r).start()
    arrived[me] = outgoing[me]
    library[grp] = mine[...]
    lax.fori_loop(1, devices, wait_a, 0)

    xf = arrived[...].astype(F32).reshape(devices, owned, CAP, width)
    xs = [xf[:, c].reshape(devices * CAP, width).astype(BF16) for c in range(owned)]
    grams = [cluster_gram(x, bands) for x in xs]
    held = {}

    def midway():
        for r in range(1, n_grp):
            lend(r).wait()
        targets = library[...].reshape(n_grp * mine.shape[0], width)
        tf = targets.astype(F32)
        held["norm"] = dot_t(jnp.ones((8, width), F32), tf * tf, HI)[0:1]
        for c, (x, g) in enumerate(zip(xs, grams)):
            u = dot_t(x, targets)
            held[c] = (u - jnp.sum(u, axis=0, keepdims=True) * (1.0 / g[2])) * g[1]

    inverses = invert_all([g[0] for g in grams], midway)
    res = []
    for c, (g, inv) in enumerate(zip(grams, inverses)):
        s = cluster_scores(held[c], held["norm"], inv, g[2], g[3], bands)
        res.append(s.reshape(devices, 1, CAP, s.shape[1]))
    full = jnp.concatenate(res, axis=1).reshape(devices, group, total)
    outbound[...] = full.astype(BF16)
    lax.fori_loop(1, devices, start_b, 0)
    returned[me] = outbound[me]
    lax.fori_loop(1, devices, wait_b, 0)
    out_ref[...] = dot_n(take_ref[...], returned[...].reshape(slots, total)).astype(BF16)


def narrow(pixels, labels, targets):
    n_tile, n_grp = lax.axis_size("tile"), lax.axis_size("grp")
    devices = n_tile * n_grp
    owned = NCLUST // devices
    group = owned * CAP
    rows, bands = pixels.shape
    width = -(-(bands + 1) // LANES) * LANES
    total = targets.shape[0] * n_grp
    vmem = pl.BlockSpec(memory_space=pltpu.VMEM)
    dma = pltpu.SemaphoreType.DMA
    return pl.pallas_call(
        functools.partial(step_body, bands, owned, n_tile, n_grp),
        out_shape=jax.ShapeDtypeStruct((rows, total), BF16),
        in_specs=[vmem] * 3,
        out_specs=vmem,
        scratch_shapes=[
            pltpu.VMEM((rows, width), BF16),
            pltpu.VMEM((devices, group, width), BF16),
            pltpu.VMEM((devices, group, width), BF16),
            pltpu.VMEM((targets.shape[0], width), BF16),
            pltpu.VMEM((n_grp, targets.shape[0], width), BF16),
            pltpu.VMEM((devices, group, total), BF16),
            pltpu.VMEM((devices, group, total), BF16),
            pltpu.VMEM((rows, NCLUST * CAP), BF16),
            dma((devices,)), dma((devices,)),
            dma((n_grp,)), dma((n_grp,)),
            dma((devices,)), dma((devices,)),
        ],
        compiler_params=pltpu.CompilerParams(
            collective_id=0, has_side_effects=True, vmem_limit_bytes=60 * 1024 * 1024
        ),
    )(labels.reshape(1, rows), pixels, targets)


def wide_cluster(pixels, labels, targets):
    n_tile = lax.axis_size("tile")
    n_grp = lax.axis_size("grp")
    band_count = pixels.shape[1]
    per_owner = 2 * NCLUST // n_tile
    target_total = targets.shape[0] * n_grp
    clusters = jnp.arange(NCLUST, dtype=jnp.int32)
    member = (labels[:, None] == clusters[None, :]).astype(jnp.int32)
    local_count = jnp.sum(member, axis=0).astype(jnp.float32)
    counts = lax.psum(local_count, ("tile", "grp"))
    place_rank = jnp.sum(jnp.cumsum(member, axis=0) * member, axis=1) - 1
    owner_pair = labels // per_owner
    inner_slot = labels % per_owner
    slot_width = CAP
    target_tile = 2 * owner_pair
    slot_index = (target_tile * per_owner + inner_slot) * slot_width + place_rank
    slot_total = n_tile * per_owner * slot_width
    outgoing = jnp.zeros((slot_total, band_count), jnp.bfloat16).at[slot_index].set(pixels)
    outgoing = outgoing.reshape(n_tile, per_owner * slot_width, band_count)
    arrived = lax.all_to_all(outgoing, "tile", split_axis=0, concat_axis=0, tiled=True)
    grouped = arrived.reshape(n_tile, per_owner, slot_width, band_count)
    gram_sum = jnp.einsum("scwb,scwd->cbd", grouped, grouped, preferred_element_type=jnp.float32)
    first_sums = jnp.sum(grouped, axis=(0, 2), dtype=jnp.float32)
    gram_sum, first_sums = lax.psum((gram_sum, first_sums), "grp")
    own_pair = lax.axis_index("tile") // 2
    own_counts = lax.dynamic_slice_in_dim(counts, own_pair * per_owner, per_owner, 0)
    own_counts = jnp.maximum(own_counts, 1.0)
    centre = first_sums / own_counts[:, None]
    identity = jnp.eye(band_count, dtype=jnp.float32)
    covariance = (
        gram_sum / own_counts[:, None, None]
        - centre[:, :, None] * centre[:, None, :]
        + 0.05 * identity
    )
    factor = jnp.linalg.cholesky(covariance)
    inverse = jax.scipy.linalg.solve_triangular(
        factor, jnp.broadcast_to(identity, factor.shape), lower=True
    )
    whitened = jnp.einsum(
        "tb,cdb->ctd",
        lax.all_gather(targets, "grp", axis=0, tiled=True).astype(jnp.float32),
        inverse,
        precision=lax.Precision.HIGHEST,
    )
    lib_norm = jnp.sum(whitened * whitened, axis=-1)
    centered = grouped.astype(jnp.float32) - centre[None, :, None, :]
    white_pix = jnp.einsum("scwb,cdb->scwd", centered, inverse, precision=lax.Precision.HIGHEST)
    inner_prod = jnp.einsum("scwd,ctd->scwt", white_pix, whitened, precision=lax.Precision.HIGHEST)
    pix_norm = jnp.sum(white_pix * white_pix, axis=-1)
    result = (
        band_count
        * inner_prod
        * inner_prod
        / ((lib_norm[None, :, None, :] + 1e-06) * (pix_norm[:, :, :, None] + 1e-06))
    )
    outbound = result.astype(jnp.bfloat16).reshape(n_tile, per_owner * slot_width, target_total)
    returned = lax.all_to_all(outbound, "tile", split_axis=0, concat_axis=0, tiled=True)
    flat_scores = returned.reshape(slot_total, target_total)
    return flat_scores[slot_index]


def local(pixels, labels, targets):
    devices = lax.axis_size("tile") * lax.axis_size("grp")
    if NCLUST % devices == 0 and devices * CAP <= pixels.shape[1]:
        return narrow(pixels, labels, targets)
    return wide_cluster(pixels, labels, targets)


def solution(mesh):
    return jax.shard_map(
        local,
        mesh=mesh,
        in_specs=(P(("tile", "grp"), None), P(("tile", "grp")), P("grp", None)),
        out_specs=P(("tile", "grp"), None),
        check_vma=False,
    )
```

profile of v0, /device:TPU:27, one launch (start us, length us, event | category | flops | bytes accessed | tf_op | source)
XLA Modules:
  0.0 54.6 jit_solution(9593991461954404745)
XLA Ops:
  0.0 0.0 copy-start
  0.0 1.7 %copy.5.tgt_ref = bf16[128,432]{1,0:T(8,128)(2,1)} copy(bf16[128,432]{0,1:T(8,128)(2,1)} %param.5) | data formatting | bytes 221184 | tf_op args[2]
  1.7 0.0 copy-done
  1.7 0.8 %copy.4.pix_ref = bf16[256,432]{1,0:T(8,128)(2,1)} copy(bf16[256,432]{0,1:T(8,128)(2,1)S(1)} %copy-done) | data formatting | bytes 442368 | tf_op args[0]
  2.5 50.4 %shard_map.37 = bf16[256,512]{1,0:T(8,128)(2,1)} custom-call(s32[1,256]{1,0:T(1,128)} %bitcast.1, bf16[256,432]{1,0:T(8,128)(2,1)} %copy.4.pix_ref, bf16[128,432]{1,0:T(8,128)(2,1)} %copy.5.tgt_ref), custom_call_target="tpu_custom_call" | custom-call | tf_op jit(solution)/shard_map/pallas_call | solution.py:298
  52.9 1.7 %copy.7 = bf16[256,512]{1,0:T(8,128)(2,1)} copy(bf16[256,512]{1,0:T(8,128)(2,1)} %shard_map.37) | data formatting | bytes 524288
Async XLA Ops:
  0.0 1.7 %copy-start = (bf16[256,432]{0,1:T(8,128)(2,1)S(1)}, bf16[256,432]{0,1:T(8,128)(2,1)}, u32[]{:S(2)}) copy-start(bf16[256,432]{0,1:T(8,128)(2,1)} %param.3) | copy-start | bytes 663556
where the time goes:
time: 54.8 us; the launch traced here: 54.6 us
  Pallas kernels  50.4 us (92%)
  local copies, waits for them, and re-layouts  4.21 us (8%)
    pallas_call x1, Pallas kernels, narrow(): pl.pallas_call(functools.partial(step_body, bands, owned, n_tile, n_grp),...  50.4 us
    unnamed x5, local copies, waits for them, and re-layouts  4.21 us

commit v1 on v0

v1 whole, which is shorter than its diff:
```python
import functools

import jax
import jax.numpy as jnp
from jax import lax
from jax.experimental import pallas as pl
from jax.experimental.pallas import tpu as pltpu
from jax.sharding import PartitionSpec as P

NCLUST = 64
CAP = 8
RIDGE = 0.05
EPS = 1e-06
STEP = 64
LANES = 128
SUB = 8
PIV = 4
OWNED = 2
MESH = pl.DeviceIdType.MESH
F32 = jnp.float32
BF16 = jnp.bfloat16


def dot_t(a, b):
    return lax.dot_general(a, b, (((1,), (1,)), ((), ())), preferred_element_type=F32)


def dot_0(a, b):
    return lax.dot_general(a, b, (((0,), (0,)), ((), ())), preferred_element_type=F32)


def dot_n(a, b):
    return lax.dot_general(a, b, (((1,), (0,)), ((), ())), preferred_element_type=F32)


def halves(v):
    big = v.astype(BF16)
    return big, (v - big.astype(F32)).astype(BF16)


def thirds(v):
    big, rest = v.astype(BF16), v
    rest = rest - big.astype(F32)
    mid = rest.astype(BF16)
    return big, mid, (rest - mid.astype(F32)).astype(BF16)


def six_left(t, axis):
    return jnp.concatenate([t[0], t[0], t[1], t[0], t[1], t[2]], axis=axis)


def six_right(t, axis):
    return jnp.concatenate([t[0], t[1], t[0], t[2], t[1], t[0]], axis=axis)


def pair_rows(t, c):
    zero = jnp.zeros_like(t)
    return jnp.concatenate([zero] * c + [t] + [zero] * (OWNED - 1 - c), axis=0)


def grow(v, rows, width):
    if v.shape[1] < width:
        v = jnp.concatenate([v, jnp.zeros((v.shape[0], width - v.shape[1]), v.dtype)], axis=1)
    if v.shape[0] < rows:
        v = jnp.concatenate([v, jnp.zeros((rows - v.shape[0], v.shape[1]), v.dtype)], axis=0)
    return v


def pivot_inverse(e):
    r = 1.0 / (e[0][0] * e[1][1] - e[0][1] * e[0][1])
    i00, i01, i11 = e[1][1] * r, -e[0][1] * r, e[0][0] * r
    x00 = i00 * e[0][2] + i01 * e[1][2]
    x01 = i00 * e[0][3] + i01 * e[1][3]
    x10 = i01 * e[0][2] + i11 * e[1][2]
    x11 = i01 * e[0][3] + i11 * e[1][3]
    s00 = e[2][2] - (e[0][2] * x00 + e[1][2] * x10)
    s01 = e[2][3] - (e[0][2] * x01 + e[1][2] * x11)
    s11 = e[3][3] - (e[0][3] * x01 + e[1][3] * x11)
    q = 1.0 / (s00 * s11 - s01 * s01)
    t00, t01, t11 = s11 * q, -s01 * q, s00 * q
    y00 = -(x00 * t00 + x01 * t01)
    y01 = -(x00 * t01 + x01 * t11)
    y10 = -(x10 * t00 + x11 * t01)
    y11 = -(x10 * t01 + x11 * t11)
    n00 = i00 - (y00 * x00 + y01 * x01)
    n01 = i01 - (y00 * x10 + y01 * x11)
    n11 = i11 - (y10 * x10 + y11 * x11)
    return [[n00, n01, y00, y01], [n01, n11, y10, y11], [y00, y10, t00, t01], [y01, y11, t01, t11]]


def paired_inverse(tile):
    rows = tile.shape[0]
    lanes = lax.broadcasted_iota(jnp.int32, (SUB, LANES), 1)
    sub = lax.broadcasted_iota(jnp.int32, (SUB, LANES), 0)
    base = jnp.where(lanes < STEP, 0, STEP)
    inside = lanes - base
    parts = [tile[g : g + SUB] for g in range(0, rows, SUB)]
    for j in range(0, rows, PIV):
        home, at = j // SUB, j % SUB
        cols = [[jnp.take_along_axis(p, base + (j + c), axis=1) for c in range(PIV)] for p in parts]
        spread = lambda v, a: jnp.broadcast_to(v[at + a : at + a + 1, :], (SUB, LANES))
        inv = pivot_inverse([[spread(cols[home][c], a) if a <= c else None for c in range(PIV)] for a in range(PIV)])
        block = (inside >= j) & (inside < j + PIV)
        src = [jnp.where(block, jnp.where(inside == j + c, 1.0, 0.0), spread(parts[home], c)) for c in range(PIV)]
        norm = [(inv[a][0] * src[0] + inv[a][1] * src[1]) + (inv[a][2] * src[2] + inv[a][3] * src[3]) for a in range(PIV)]
        fresh = []
        for g, p in enumerate(parts):
            col = cols[g]
            rest = jnp.where(block, 0.0, p) - (
                (col[0] * norm[0] + col[1] * norm[1]) + (col[2] * norm[2] + col[3] * norm[3])
            )
            if g == home:
                for a in range(PIV):
                    rest = jnp.where(sub == at + a, norm[a], rest)
            fresh.append(rest)
        parts = fresh
    return jnp.concatenate(parts, axis=0)


class Eliminate:
    def __init__(self):
        self.inverse = [None] * OWNED
        self.k = 0

    def add(self, rows):
        k = self.k
        wide = rows[0].shape[1]
        old = -(-k * STEP // LANES) * LANES
        lane = lax.broadcasted_iota(jnp.int32, (STEP, LANES), 1)
        own = [m[:, k * STEP // LANES * LANES :][:, :LANES] for m in rows]
        odd = k % 2
        own[1 - odd] = pltpu.roll(own[1 - odd], STEP, 1)
        pair = jnp.where(lane < STEP, own[0], own[1])
        lifts = []
        if k:
            lefts, rights = [], []
            for c, m in enumerate(rows):
                r3 = thirds(m[:, :old])
                lift = dot_n(six_left(r3, 1), six_right(thirds(self.inverse[c]), 0))
                lifts.append(lift)
                lefts.append(six_left(thirds(lift), 1))
                rights.append(six_right([pair_rows(t, c) for t in r3], 1))
            pair = pair - dot_t(jnp.concatenate(lefts, axis=1), jnp.concatenate(rights, axis=1))
        pair = paired_inverse(pair)
        wl = lax.broadcasted_iota(jnp.int32, (STEP, wide), 1)
        ws = lax.broadcasted_iota(jnp.int32, (STEP, wide), 0)
        eye = jnp.where(wl == ws + k * STEP, 1.0, 0.0)
        if not k:
            turned = pltpu.roll(pair, STEP, 1)
            self.inverse = [grow(jnp.where(lane < STEP, v, 0.0), LANES, LANES) for v in (pair, turned)]
        else:
            left = six_left(thirds(pair), 1)
            for c in range(OWNED):
                q3 = thirds(eye - grow(lifts[c], STEP, wide))
                w = dot_n(left, six_right([pair_rows(t, c) for t in q3], 0))
                upd = dot_0(six_left(q3, 0), six_right(thirds(w), 0))
                self.inverse[c] = grow(self.inverse[c], wide, wide) + upd
        self.k = k + 1


def slot_of(lab, me, devices):
    count = lab.shape[1]
    ri = lax.broadcasted_iota(jnp.int32, (count, count), 0)
    ci = lax.broadcasted_iota(jnp.int32, (count, count), 1)
    lab_row = lab.astype(F32)
    lab_col = jnp.sum(jnp.where(ri == ci, lab_row, 0.0), axis=1, keepdims=True)
    same = jnp.where(lab_row == lab_col, 1.0, 0.0)
    rank_col = jnp.sum(jnp.where(ci < ri, same, 0.0), axis=1, keepdims=True).astype(jnp.int32)
    rank_row = jnp.sum(jnp.where(ri < ci, same, 0.0), axis=0, keepdims=True).astype(jnp.int32)
    lab_col = lab_col.astype(jnp.int32)
    hop = lambda v: jnp.bitwise_xor(lax.shift_right_logical(v, 1), me)
    side = lambda v: jnp.bitwise_and(v, 1)
    slots = devices * CAP
    down = lax.broadcasted_iota(jnp.int32, (slots, count), 0)
    put = [
        jnp.where(down == jnp.where(side(lab) == c, hop(lab) * CAP + rank_row, -1), 1.0, 0.0).astype(BF16)
        for c in range(OWNED)
    ]
    across = lax.broadcasted_iota(jnp.int32, (count, slots * OWNED), 1)
    take = jnp.where(across == (hop(lab_col) * OWNED + side(lab_col)) * CAP + rank_col, 1.0, 0.0).astype(BF16)
    far = lax.broadcasted_iota(jnp.int32, (devices, count), 0)
    lane = lax.broadcasted_iota(jnp.int32, (count, LANES), 1)
    near = jnp.where(lax.div(lane, STEP) == side(lab_col), 1.0, 0.0).astype(BF16)
    tally = dot_n(jnp.where(far == hop(lab), 1.0, 0.0).astype(BF16), near)
    return take, put, tally


def step_body(
    bands, n_tile, n_grp,
    lab_ref, pix_ref, tgt_ref, out_ref,
    outgoing, arrived, counts, heard, library, outbound, returned, take_ref,
    send_n, recv_n, send_a, recv_a, send_t, recv_t, send_b, recv_b,
):
    devices = n_tile * n_grp
    full, rest = bands // LANES, bands % LANES
    flag = OWNED * rest
    total = outbound.shape[2]
    size = devices * CAP
    blocks = size // STEP
    span = STEP // CAP
    tile = lax.axis_index("tile")
    grp = lax.axis_index("grp")
    me = tile * n_grp + grp

    def flip(v, r):
        out = v
        for k in range(r.bit_length()):
            if (r >> k) & 1:
                out = out + (1 - 2 * lax.rem(lax.div(v, 1 << k), 2)) * (1 << k)
        return out

    def place(r):
        return (flip(tile, r // n_grp), flip(grp, r % n_grp))

    barrier = pltpu.get_barrier_semaphore()
    for r in range(devices - 1, 0, -1):
        pl.semaphore_signal(barrier, inc=1, device_id=place(r), device_id_type=MESH)

    take, put, tally = slot_of(lab_ref[...], me, devices)
    take_ref[...] = take
    counts[...] = tally.reshape(devices, 1, LANES)
    heard[0] = counts[0]
    for c in range(OWNED):
        body = dot_t(put[c], pix_ref[: full * LANES, :])
        for t in range(full):
            at = (c * full + t) * SUB
            outgoing[:, at : at + SUB, :] = body[:, t * LANES : (t + 1) * LANES].astype(BF16).reshape(devices, SUB, LANES)
    tail = pix_ref[full * LANES :, :]
    pad = LANES - flag
    mark = lax.broadcasted_iota(jnp.int32, (pad, tail.shape[1]), 0)
    ends = [
        jnp.concatenate(
            [tail if i == c else jnp.zeros_like(tail) for i in range(OWNED)]
            + [jnp.where(mark == c, 1.0, 0.0).astype(BF16)],
            axis=0,
        )
        for c in range(OWNED)
    ]
    ends = dot_t(jnp.concatenate(put, axis=1), jnp.concatenate(ends, axis=1))
    outgoing[:, OWNED * full * SUB :, :] = ends.astype(BF16).reshape(devices, SUB, LANES)
    arrived[0] = outgoing[0]
    library[grp] = tgt_ref[...]
    pl.semaphore_wait(barrier, devices - 1)

    def ship(src, dst, sends, recvs, r):
        return pltpu.make_async_remote_copy(
            src_ref=src.at[r], dst_ref=dst.at[r],
            send_sem=sends.at[r], recv_sem=recvs.at[r],
            device_id=place(r), device_id_type=MESH,
        )

    tell = lambda r: ship(counts, heard, send_n, recv_n, r)
    go = lambda r: ship(outgoing, arrived, send_a, recv_a, r)
    back = lambda r: ship(outbound, returned, send_b, recv_b, r)

    def lend(i, src, home, to):
        return pltpu.make_async_remote_copy(
            src_ref=src, dst_ref=library.at[home], send_sem=send_t.at[i], recv_sem=recv_t.at[i],
            device_id=(tile, flip(grp, to)), device_id_type=MESH,
        )

    across = flip(grp, 2)
    lends = [lend(0, tgt_ref, grp, 1), lend(1, tgt_ref, grp, 2), lend(2, library.at[across], across, 1)]
    half = devices // 2
    for r in range(devices - 1, 0, -1):
        tell(r).start()
    for r in range(half):
        go(half + r).start()
        if r:
            go(r).start()
    lends[0].start()
    lends[1].start()

    lane = lax.broadcasted_iota(jnp.int32, (STEP, LANES), 1)
    own = [((lane >= c * rest) & (lane < (c + 1) * rest)) for c in range(OWNED)]
    kept = [own[c] | (lane == flag + c) for c in range(OWNED)]
    sign = lax.broadcasted_iota(jnp.int32, (16, (full + 1) * LANES), 1)
    sign = [jnp.where(sign == full * LANES + flag + c, 1.0, 0.0).astype(BF16) for c in range(OWNED)]
    lefts = [[] for _ in range(OWNED)]
    rights = [[] for _ in range(OWNED)]
    valid = [[] for _ in range(OWNED)]
    centre = [None] * OWNED
    state = Eliminate()
    number = None
    held = {}

    def load(b):
        arr = arrived[b * span : (b + 1) * span].astype(F32)
        cut = lambda i: arr[:, i * SUB : (i + 1) * SUB, :].reshape(STEP, LANES)
        edge = cut(OWNED * full)
        out = []
        for c in range(OWNED):
            main = [cut(c * full + t) for t in range(full)]
            x = jnp.concatenate(main + [edge], axis=1)
            if b == 0:
                tops = jnp.maximum(jnp.sum(edge[:, flag + c : flag + c + 1]), 1.0)
                mid = jnp.concatenate(main + [jnp.where(own[c], edge, 0.0)], axis=1)
                mid = jnp.sum(mid, axis=0, keepdims=True) * (1.0 / tops)
                mid = mid.astype(BF16)
                centre[c] = (mid, mid.astype(F32))
            lefts[c].append(x.astype(BF16))
            rights[c].append(jnp.concatenate(main + [jnp.where(kept[c], edge, 0.0)], axis=1).astype(BF16))
            valid[c].append(edge[:, flag + c : flag + c + 1])
            out.append(jnp.sum(x * centre[c][1], axis=1, keepdims=True))
        return out

    def gram(b, lean):
        rows = []
        wide = -(-(b + 1) * STEP // LANES) * LANES
        for c in range(OWNED):
            mid, midf = centre[c]
            left = jnp.concatenate([lefts[c][b], jnp.broadcast_to(mid, (16, mid.shape[1])), sign[c]], axis=0)
            right = jnp.concatenate(rights[c], axis=0)
            if right.shape[0] < wide:
                right = jnp.concatenate([right, jnp.zeros((wide - right.shape[0], right.shape[1]), BF16)], axis=0)
            g = dot_t(left, right)
            along, has = g[STEP : STEP + 1], g[STEP + 16 : STEP + 17]
            along = along - jnp.sum(midf * midf) * has
            rows.append(g[:STEP] - valid[c][b] * along - lean[c] * has)
        return rows

    def scale(b, rows):
        wide = rows[0].shape[1]
        wl = lax.broadcasted_iota(jnp.int32, (STEP, wide), 1)
        ws = lax.broadcasted_iota(jnp.int32, (STEP, wide), 0)
        diag = wl == ws + b * STEP
        return [m + jnp.where(diag, number[c] * RIDGE, 0.0) for c, m in enumerate(rows)]

    for b in range(blocks):
        for r in range(b * span, (b + 1) * span):
            if r:
                go(r).wait_recv()
        rows = gram(b, load(b))
        if b == 0:
            for r in range(1, devices):
                tell(r).wait_recv()
            heads = jnp.maximum(jnp.sum(heard[...], axis=0), 1.0)
            number = [heads[:, c * STEP : c * STEP + 1] for c in range(OWNED)]
        if b == 1:
            lends[1].wait_recv()
            lends[2].start()
        if b == blocks - 1:
            for i in (0, 2):
                lends[i].wait_recv()
            targets = jnp.concatenate([library[i] for i in range(n_grp)], axis=1)
            tf = targets.astype(F32)
            held["norm"] = jnp.sum(tf * tf, axis=0, keepdims=True)
            zero = jnp.zeros((rest, total), BF16)
            for c in range(OWNED):
                lib = [targets[: full * LANES]]
                lib += [targets[full * LANES :] if i == c else zero for i in range(OWNED)]
                lib += [jnp.zeros((pad, total), BF16)]
                u = dot_n(jnp.concatenate(lefts[c], axis=0), jnp.concatenate(lib, axis=0))
                v = jnp.concatenate(valid[c], axis=0)
                held[c] = (u - jnp.sum(u, axis=0, keepdims=True) * (1.0 / number[c])) * v
        state.add(scale(b, rows))

    diag = lax.broadcasted_iota(jnp.int32, (LANES, LANES), 0) == lax.broadcasted_iota(jnp.int32, (LANES, LANES), 1)
    res = []
    for c in range(OWNED):
        inv, u, n = state.inverse[c], held[c], number[c]
        i1, i2, i3 = thirds(inv)
        u1, u2 = halves(u)
        z = dot_n(jnp.concatenate([i1, i1, i2], axis=1), jnp.concatenate([u1, u2, u1], axis=0))
        v = jnp.broadcast_to(jnp.concatenate(valid[c], axis=0), (size, LANES)).astype(BF16)
        p = dot_n(jnp.concatenate([i1, i2, i3], axis=1), jnp.concatenate([v, v, v], axis=0))
        s = jnp.sum(p, axis=0, keepdims=True)
        s = jnp.where(s > 0.0, 1.0 / jnp.where(s > 0.0, s, 1.0), 0.0)
        w = jnp.sum(z, axis=0, keepdims=True)
        ws = w * s[:, 0:1]
        lib = (held["norm"] - jnp.sum(u * z, axis=0, keepdims=True) + w * ws) * (1.0 / RIDGE)
        lib = jnp.maximum(lib, 0.0) + EPS
        kd = jnp.concatenate(
            [
                jnp.sum(jnp.where(diag, inv[i : i + LANES, i : i + LANES], 0.0), axis=1, keepdims=True)
                for i in range(0, size, LANES)
            ],
            axis=0,
        )
        kd = kd - p * p * s
        pix = n * (1.0 - (n * RIDGE) * kd) - 1.0
        pix = jnp.maximum(pix, 0.0) + EPS
        gain = (n * n * bands) / pix
        lib = 1.0 / lib
        pieces = []
        for i in range(0, total, LANES):
            d = z[:, i : i + LANES] - p * ws[:, i : i + LANES]
            pieces.append(d * d * gain * lib[:, i : i + LANES])
        res.append(jnp.concatenate(pieces, axis=1).reshape(devices, 1, CAP, total))
    joined = jnp.concatenate(res, axis=1).reshape(devices, OWNED * CAP, total).astype(BF16)
    for lo, hi in ((half, devices), (0, half)):
        outbound[lo:hi] = joined[lo:hi]
        for r in range(hi - 1, max(lo, 1) - 1, -1):
            back(r).start()
    returned[0] = outbound[0]
    for r in range(1, devices):
        tell(r).wait_send()
        go(r).wait_send()
    for cp in lends:
        cp.wait_send()
    for r in range(1, devices):
        back(r).wait()
    out_ref[...] = dot_n(take_ref[...], returned[...].reshape(size * OWNED, total)).astype(BF16)


def narrow(pixels, labels, targets):
    n_tile, n_grp = lax.axis_size("tile"), lax.axis_size("grp")
    devices = n_tile * n_grp
    rows, bands = pixels.shape
    total = targets.shape[0] * n_grp
    deep = (OWNED * (bands // LANES) + 1) * SUB
    vmem = pl.BlockSpec(memory_space=pltpu.VMEM)
    dma = pltpu.SemaphoreType.DMA
    return pl.pallas_call(
        functools.partial(step_body, bands, n_tile, n_grp),
        out_shape=jax.ShapeDtypeStruct((rows, total), BF16),
        in_specs=[vmem] * 3,
        out_specs=vmem,
        scratch_shapes=[
            pltpu.VMEM((devices, deep, LANES), BF16),
            pltpu.VMEM((devices, deep, LANES), BF16),
            pltpu.VMEM((devices, 1, LANES), F32),
            pltpu.VMEM((devices, 1, LANES), F32),
            pltpu.VMEM((n_grp, bands, targets.shape[0]), BF16),
            pltpu.VMEM((devices, OWNED * CAP, total), BF16),
            pltpu.VMEM((devices, OWNED * CAP, total), BF16),
            pltpu.VMEM((rows, NCLUST * CAP), BF16),
            dma((devices,)), dma((devices,)),
            dma((devices,)), dma((devices,)),
            dma((n_grp,)), dma((n_grp,)),
            dma((devices,)), dma((devices,)),
        ],
        compiler_params=pltpu.CompilerParams(
            collective_id=0, has_side_effects=True, vmem_limit_bytes=60 * 1024 * 1024
        ),
    )(labels.reshape(1, rows), pixels.T, targets.T)


def wide_cluster(pixels, labels, targets):
    n_tile = lax.axis_size("tile")
    n_grp = lax.axis_size("grp")
    band_count = pixels.shape[1]
    per_owner = 2 * NCLUST // n_tile
    target_total = targets.shape[0] * n_grp
    clusters = jnp.arange(NCLUST, dtype=jnp.int32)
    member = (labels[:, None] == clusters[None, :]).astype(jnp.int32)
    local_count = jnp.sum(member, axis=0).astype(jnp.float32)
    counts = lax.psum(local_count, ("tile", "grp"))
    place_rank = jnp.sum(jnp.cumsum(member, axis=0) * member, axis=1) - 1
    owner_pair = labels // per_owner
    inner_slot = labels % per_owner
    slot_width = CAP
    target_tile = 2 * owner_pair
    slot_index = (target_tile * per_owner + inner_slot) * slot_width + place_rank
    slot_total = n_tile * per_owner * slot_width
    outgoing = jnp.zeros((slot_total, band_count), jnp.bfloat16).at[slot_index].set(pixels)
    outgoing = outgoing.reshape(n_tile, per_owner * slot_width, band_count)
    arrived = lax.all_to_all(outgoing, "tile", split_axis=0, concat_axis=0, tiled=True)
    grouped = arrived.reshape(n_tile, per_owner, slot_width, band_count)
    gram_sum = jnp.einsum("scwb,scwd->cbd", grouped, grouped, preferred_element_type=jnp.float32)
    first_sums = jnp.sum(grouped, axis=(0, 2), dtype=jnp.float32)
    gram_sum, first_sums = lax.psum((gram_sum, first_sums), "grp")
    own_pair = lax.axis_index("tile") // 2
    own_counts = lax.dynamic_slice_in_dim(counts, own_pair * per_owner, per_owner, 0)
    own_counts = jnp.maximum(own_counts, 1.0)
    centre = first_sums / own_counts[:, None]
    identity = jnp.eye(band_count, dtype=jnp.float32)
    covariance = (
        gram_sum / own_counts[:, None, None]
        - centre[:, :, None] * centre[:, None, :]
        + 0.05 * identity
    )
    factor = jnp.linalg.cholesky(covariance)
    inverse = jax.scipy.linalg.solve_triangular(
        factor, jnp.broadcast_to(identity, factor.shape), lower=True
    )
    whitened = jnp.einsum(
        "tb,cdb->ctd",
        lax.all_gather(targets, "grp", axis=0, tiled=True).astype(jnp.float32),
        inverse,
        precision=lax.Precision.HIGHEST,
    )
    lib_norm = jnp.sum(whitened * whitened, axis=-1)
    centered = grouped.astype(jnp.float32) - centre[None, :, None, :]
    white_pix = jnp.einsum("scwb,cdb->scwd", centered, inverse, precision=lax.Precision.HIGHEST)
    inner_prod = jnp.einsum("scwd,ctd->scwt", white_pix, whitened, precision=lax.Precision.HIGHEST)
    pix_norm = jnp.sum(white_pix * white_pix, axis=-1)
    result = (
        band_count
        * inner_prod
        * inner_prod
        / ((lib_norm[None, :, None, :] + 1e-06) * (pix_norm[:, :, :, None] + 1e-06))
    )
    outbound = result.astype(jnp.bfloat16).reshape(n_tile, per_owner * slot_width, target_total)
    returned = lax.all_to_all(outbound, "tile", split_axis=0, concat_axis=0, tiled=True)
    flat_scores = returned.reshape(slot_total, target_total)
    return flat_scores[slot_index]


def local(pixels, labels, targets):
    n_tile, n_grp = lax.axis_size("tile"), lax.axis_size("grp")
    devices = n_tile * n_grp
    rest = pixels.shape[1] % LANES
    if (
        NCLUST == OWNED * devices
        and n_grp == 4
        and n_tile & (n_tile - 1) == 0
        and devices * CAP % (2 * STEP) == 0
        and rest % 16 == 0
        and OWNED * (rest + 1) <= LANES
    ):
        return narrow(pixels, labels, targets)
    return wide_cluster(pixels, labels, targets)


def solution(mesh):
    return jax.shard_map(
        local,
        mesh=mesh,
        in_specs=(P(("tile", "grp"), None), P(("tile", "grp")), P("grp", None)),
        out_specs=P(("tile", "grp"), None),
        check_vma=False,
    )
```

time: 54.8 us -> 46.4 us (0.85)
  the two profiles are of different devices: /device:TPU:27 before, /device:TPU:0 now
where the time goes in v1:
time: 46.4 us; the launch traced here: 46.3 us
  Pallas kernels  44.6 us (96%)
  local copies, waits for them, and re-layouts  1.67 us (4%)
    pallas_call x1, Pallas kernels, narrow(): pl.pallas_call(functools.partial(step_body, bands, n_tile, n_grp), out_sh...  44.6 us
    unnamed x1, local copies, waits for them, and re-layouts  1.67 us

profile of v1, /device:TPU:0, one launch (start us, length us, event | category | flops | bytes accessed | tf_op | source)
XLA Modules:
  0.0 46.3 jit_solution(12408931911795385319)
XLA Ops:
  0.0 44.6 %shard_map.37 = bf16[256,512]{1,0:T(8,128)(2,1)} custom-call(s32[1,256]{1,0:T(1,128)} %bitcast.5, bf16[432,256]{1,0:T(8,128)(2,1)} %bitcast.3, bf16[432,128]{1,0:T(8,128)(2,1)} %bitcast.4), custom_call_target="tpu_custom_call" | custom-call | tf_op jit(solution)/shard_map/pallas_call | solution.py:414
  44.6 1.7 %copy.5 = bf16[256,512]{1,0:T(8,128)(2,1)} copy(bf16[256,512]{1,0:T(8,128)(2,1)} %shard_map.37) | data formatting | bytes 524288

commit v2 on v1

--- a/solution.py
+++ b/solution.py
@@ -88,33 +88,41 @@
     return [[n00, n01, y00, y01], [n01, n11, y10, y11], [y00, y10, t00, t01], [y01, y11, t01, t11]]
 
 
-def paired_inverse(tile):
+def paired_factor(tile, fill):
     rows = tile.shape[0]
     lanes = lax.broadcasted_iota(jnp.int32, (SUB, LANES), 1)
     sub = lax.broadcasted_iota(jnp.int32, (SUB, LANES), 0)
     base = jnp.where(lanes < STEP, 0, STEP)
     inside = lanes - base
     parts = [tile[g : g + SUB] for g in range(0, rows, SUB)]
+    low, scaled = [], []
     for j in range(0, rows, PIV):
         home, at = j // SUB, j % SUB
-        cols = [[jnp.take_along_axis(p, base + (j + c), axis=1) for c in range(PIV)] for p in parts]
+        pick = lambda p: [jnp.take_along_axis(p, base + (j + c), axis=1) for c in range(PIV)]
         spread = lambda v, a: jnp.broadcast_to(v[at + a : at + a + 1, :], (SUB, LANES))
-        inv = pivot_inverse([[spread(cols[home][c], a) if a <= c else None for c in range(PIV)] for a in range(PIV)])
+        first = pick(parts[home])
+        inv = pivot_inverse([[spread(first[c], a) if a <= c else None for c in range(PIV)] for a in range(PIV)])
         block = (inside >= j) & (inside < j + PIV)
         src = [jnp.where(block, jnp.where(inside == j + c, 1.0, 0.0), spread(parts[home], c)) for c in range(PIV)]
         norm = [(inv[a][0] * src[0] + inv[a][1] * src[1]) + (inv[a][2] * src[2] + inv[a][3] * src[3]) for a in range(PIV)]
-        fresh = []
-        for g, p in enumerate(parts):
-            col = cols[g]
-            rest = jnp.where(block, 0.0, p) - (
+        if not at:
+            low.append(jnp.zeros((SUB, LANES), F32))
+            scaled.append(jnp.zeros((SUB, LANES), F32))
+        done = inside < j + PIV
+        for a in range(PIV):
+            here = (sub == at + a) & done
+            low[home] = jnp.where(here, src[a], low[home])
+            scaled[home] = jnp.where(here, norm[a], scaled[home])
+        for g in range(home if at + PIV < SUB else home + 1, rows // SUB):
+            col = first if g == home else pick(parts[g])
+            parts[g] = jnp.where(block, 0.0, parts[g]) - (
                 (col[0] * norm[0] + col[1] * norm[1]) + (col[2] * norm[2] + col[3] * norm[3])
             )
-            if g == home:
-                for a in range(PIV):
-                    rest = jnp.where(sub == at + a, norm[a], rest)
-            fresh.append(rest)
-        parts = fresh
-    return jnp.concatenate(parts, axis=0)
+        if fill:
+            fill.pop(0)()
+    while fill:
+        fill.pop(0)()
+    return jnp.concatenate(low + scaled, axis=0)
 
 
 class Eliminate:
@@ -122,7 +130,7 @@
         self.inverse = [None] * OWNED
         self.k = 0
 
-    def add(self, rows):
+    def reduce(self, rows):
         k = self.k
         wide = rows[0].shape[1]
         old = -(-k * STEP // LANES) * LANES
@@ -131,31 +139,34 @@
         odd = k % 2
         own[1 - odd] = pltpu.roll(own[1 - odd], STEP, 1)
         pair = jnp.where(lane < STEP, own[0], own[1])
-        lifts = []
-        if k:
-            lefts, rights = [], []
-            for c, m in enumerate(rows):
-                r3 = thirds(m[:, :old])
-                lift = dot_n(six_left(r3, 1), six_right(thirds(self.inverse[c]), 0))
-                lifts.append(lift)
-                lefts.append(six_left(thirds(lift), 1))
-                rights.append(six_right([pair_rows(t, c) for t in r3], 1))
-            pair = pair - dot_t(jnp.concatenate(lefts, axis=1), jnp.concatenate(rights, axis=1))
-        pair = paired_inverse(pair)
         wl = lax.broadcasted_iota(jnp.int32, (STEP, wide), 1)
         ws = lax.broadcasted_iota(jnp.int32, (STEP, wide), 0)
         eye = jnp.where(wl == ws + k * STEP, 1.0, 0.0)
         if not k:
-            turned = pltpu.roll(pair, STEP, 1)
-            self.inverse = [grow(jnp.where(lane < STEP, v, 0.0), LANES, LANES) for v in (pair, turned)]
-        else:
-            left = six_left(thirds(pair), 1)
-            for c in range(OWNED):
-                q3 = thirds(eye - grow(lifts[c], STEP, wide))
-                w = dot_n(left, six_right([pair_rows(t, c) for t in q3], 0))
-                upd = dot_0(six_left(q3, 0), six_right(thirds(w), 0))
-                self.inverse[c] = grow(self.inverse[c], wide, wide) + upd
-        self.k = k + 1
+            return pair, [eye] * OWNED
+        lefts, rights, maps = [], [], []
+        for c, m in enumerate(rows):
+            r3 = thirds(m[:, :old])
+            lift = dot_n(six_left(r3, 1), six_right(thirds(self.inverse[c]), 0))
+            maps.append(eye - grow(lift, STEP, wide))
+            lefts.append(six_left(thirds(lift), 1))
+            rights.append(six_right([pair_rows(t, c) for t in r3], 1))
+        return pair - dot_t(jnp.concatenate(lefts, axis=1), jnp.concatenate(rights, axis=1)), maps
+
+    def extend(self, factor, maps):
+        wide = maps[0].shape[1]
+        lane = lax.broadcasted_iota(jnp.int32, factor.shape, 1)
+        left = None if not self.k else six_left(thirds(factor), 1)
+        for c in range(OWNED):
+            if not self.k:
+                both = factor if not c else pltpu.roll(factor, STEP, 1)
+                both = jnp.where(lane < STEP, both, 0.0)
+            else:
+                q3 = thirds(maps[c])
+                both = dot_n(left, six_right([pair_rows(t, c) for t in q3], 0))
+            upd = dot_0(six_left(thirds(both[:STEP]), 0), six_right(thirds(both[STEP:]), 0))
+            self.inverse[c] = upd if not self.k else grow(self.inverse[c], wide, wide) + upd
+        self.k += 1
 
 
 def slot_of(lab, me, devices):
@@ -262,12 +273,13 @@
     across = flip(grp, 2)
     lends = [lend(0, tgt_ref, grp, 1), lend(1, tgt_ref, grp, 2), lend(2, library.at[across], across, 1)]
     half = devices // 2
+    late = devices - span
     for r in range(devices - 1, 0, -1):
         tell(r).start()
-    for r in range(half):
-        go(half + r).start()
-        if r:
-            go(r).start()
+    for r in range(1, half):
+        go(r).start()
+    for r in range(half, late):
+        go(r).start()
     lends[0].start()
     lends[1].start()
 
@@ -326,66 +338,109 @@
         diag = wl == ws + b * STEP
         return [m + jnp.where(diag, number[c] * RIDGE, 0.0) for c, m in enumerate(rows)]
 
+    def fetch(b):
+        for r in range(max(b * span, 1), (b + 1) * span):
+            go(r).wait_recv()
+        return load(b)
+
+    def measure(c):
+        def run():
+            lib = [held["lib"][: full * LANES]]
+            lib += [held["lib"][full * LANES :] if i == c else jnp.zeros((rest, total), BF16) for i in range(OWNED)]
+            lib += [jnp.zeros((pad, total), BF16)]
+            u = dot_n(jnp.concatenate(lefts[c], axis=0), jnp.concatenate(lib, axis=0))
+            v = jnp.concatenate(valid[c], axis=0)
+            u = (u - jnp.sum(u, axis=0, keepdims=True) * (1.0 / number[c])) * v
+            held[c] = jnp.concatenate([u, jnp.broadcast_to(v, (size, LANES))], axis=1)
+
+        return run
+
+    def advance(c):
+        def run():
+            u1, u2 = halves(held[c])
+            m1, m2 = halves(jnp.concatenate([state.inverse[c][: size - STEP], held["maps"][c]], axis=0))
+            z = dot_n(jnp.concatenate([m1, m1, m2], axis=1), jnp.concatenate([u1, u2, u1], axis=0))
+            held["z", c] = z[: size - STEP]
+            held["q", c] = z[size - STEP :]
+
+        return run
+
+    def summarise(c):
+        def run():
+            z = held["z", c]
+            held["lib", c] = jnp.sum(held[c][: size - STEP] * z, axis=0, keepdims=True)
+            held["sum", c] = jnp.sum(z, axis=0, keepdims=True)
+            inv = state.inverse[c]
+            held["diag", c] = [
+                jnp.sum(jnp.where(diag, inv[i : i + LANES, i : i + LANES], 0.0), axis=1, keepdims=True)
+                for i in range(0, size, LANES)
+            ]
+
+        return run
+
+    def squares():
+        tf = held["lib"].astype(F32)
+        held["norm"] = jnp.sum(tf * tf, axis=0, keepdims=True)
+
+    diag = lax.broadcasted_iota(jnp.int32, (LANES, LANES), 0) == lax.broadcasted_iota(jnp.int32, (LANES, LANES), 1)
+    rows = gram(0, fetch(0))
+    for r in range(1, devices):
+        tell(r).wait_recv()
+    heads = jnp.maximum(jnp.sum(heard[...], axis=0), 1.0)
+    number = [heads[:, c * STEP : c * STEP + 1] for c in range(OWNED)]
+    for r in range(late, devices):
+        go(r).start()
     for b in range(blocks):
-        for r in range(b * span, (b + 1) * span):
-            if r:
-                go(r).wait_recv()
-        rows = gram(b, load(b))
-        if b == 0:
-            for r in range(1, devices):
-                tell(r).wait_recv()
-            heads = jnp.maximum(jnp.sum(heard[...], axis=0), 1.0)
-            number = [heads[:, c * STEP : c * STEP + 1] for c in range(OWNED)]
-        if b == 1:
-            lends[1].wait_recv()
-            lends[2].start()
-        if b == blocks - 1:
-            for i in (0, 2):
-                lends[i].wait_recv()
-            targets = jnp.concatenate([library[i] for i in range(n_grp)], axis=1)
-            tf = targets.astype(F32)
-            held["norm"] = jnp.sum(tf * tf, axis=0, keepdims=True)
-            zero = jnp.zeros((rest, total), BF16)
-            for c in range(OWNED):
-                lib = [targets[: full * LANES]]
-                lib += [targets[full * LANES :] if i == c else zero for i in range(OWNED)]
-                lib += [jnp.zeros((pad, total), BF16)]
-                u = dot_n(jnp.concatenate(lefts[c], axis=0), jnp.concatenate(lib, axis=0))
-                v = jnp.concatenate(valid[c], axis=0)
-                held[c] = (u - jnp.sum(u, axis=0, keepdims=True) * (1.0 / number[c])) * v
-        state.add(scale(b, rows))
-
-    diag = lax.broadcasted_iota(jnp.int32, (LANES, LANES), 0) == lax.broadcasted_iota(jnp.int32, (LANES, LANES), 1)
+        pair, maps = state.reduce(scale(b, rows))
+        if b < blocks - 1:
+            factor = paired_factor(pair, [])
+            state.extend(factor, maps)
+            lean = fetch(b + 1)
+            rows = gram(b + 1, lean)
+            if not b:
+                lends[1].wait_recv()
+                lends[2].start()
+    held["maps"] = maps
+    for i in (0, 2):
+        lends[i].wait_recv()
+    held["lib"] = jnp.concatenate([library[i] for i in range(n_grp)], axis=1)
+    state.inverse = [grow(m, size, size) for m in state.inverse]
+    fill = [measure(0), measure(1), squares, advance(0), advance(1), summarise(0), summarise(1)]
+    factor = paired_factor(pair, fill)
+
+    f1, f2 = halves(factor)
+    left = jnp.concatenate([f1, f1, f2], axis=1)
     res = []
     for c in range(OWNED):
-        inv, u, n = state.inverse[c], held[c], number[c]
-        i1, i2, i3 = thirds(inv)
-        u1, u2 = halves(u)
-        z = dot_n(jnp.concatenate([i1, i1, i2], axis=1), jnp.concatenate([u1, u2, u1], axis=0))
-        v = jnp.broadcast_to(jnp.concatenate(valid[c], axis=0), (size, LANES)).astype(BF16)
-        p = dot_n(jnp.concatenate([i1, i2, i3], axis=1), jnp.concatenate([v, v, v], axis=0))
-        s = jnp.sum(p, axis=0, keepdims=True)
+        n = number[c]
+        m1, m2 = halves(jnp.concatenate([held["q", c], maps[c]], axis=1))
+        both = dot_n(left, jnp.concatenate([pair_rows(t, c) for t in (m1, m2, m1)], axis=0))
+        gu, g = both[:STEP, : total + LANES], both[:STEP, total + LANES :]
+        nu, d = both[STEP:, : total + LANES], both[STEP:, total + LANES :]
+        g1, g2 = halves(g)
+        n1, n2 = halves(nu)
+        z = dot_0(jnp.concatenate([g1, g1, g2], axis=0), jnp.concatenate([n1, n2, n1], axis=0))
+        z = jnp.concatenate([held["z", c] + z[: size - STEP], z[size - STEP :]], axis=0)
+        energy = held["lib", c] + jnp.sum(gu * nu, axis=0, keepdims=True)
+        w = held["sum", c][:, :total] + jnp.sum(
+            jnp.concatenate([gu[:, total:]] * (total // LANES), axis=1) * nu[:, :total], axis=0, keepdims=True
+        )
+        kd = thirds(g * d)
+        kd = dot_0(jnp.concatenate(kd, axis=0), jnp.ones((3 * STEP, LANES), BF16))
+        kd = kd + jnp.concatenate(held["diag", c], axis=0)
+        p = z[:, total:]
+        s = energy[:, total:]
         s = jnp.where(s > 0.0, 1.0 / jnp.where(s > 0.0, s, 1.0), 0.0)
-        w = jnp.sum(z, axis=0, keepdims=True)
         ws = w * s[:, 0:1]
-        lib = (held["norm"] - jnp.sum(u * z, axis=0, keepdims=True) + w * ws) * (1.0 / RIDGE)
-        lib = jnp.maximum(lib, 0.0) + EPS
-        kd = jnp.concatenate(
-            [
-                jnp.sum(jnp.where(diag, inv[i : i + LANES, i : i + LANES], 0.0), axis=1, keepdims=True)
-                for i in range(0, size, LANES)
-            ],
-            axis=0,
-        )
+        lib = (held["norm"] - energy[:, :total] + w * ws) * (1.0 / RIDGE)
+        lib = 1.0 / (jnp.maximum(lib, 0.0) + EPS)
         kd = kd - p * p * s
         pix = n * (1.0 - (n * RIDGE) * kd) - 1.0
-        pix = jnp.maximum(pix, 0.0) + EPS
-        gain = (n * n * bands) / pix
-        lib = 1.0 / lib
+        gain = (n * n * bands) / (jnp.maximum(pix, 0.0) + EPS)
         pieces = []
         for i in range(0, total, LANES):
-            d = z[:, i : i + LANES] - p * ws[:, i : i + LANES]
-            pieces.append(d * d * gain * lib[:, i : i + LANES])
+            e = z[:, i : i + LANES] - p * ws[:, i : i + LANES]
+            pieces.append(e * e * gain * lib[:, i : i + LANES])
         res.append(jnp.concatenate(pieces, axis=1).reshape(devices, 1, CAP, total))
     joined = jnp.concatenate(res, axis=1).reshape(devices, OWNED * CAP, total).astype(BF16)
     for lo, hi in ((half, devices), (0, half)):

time: 46.4 us -> 44.9 us (0.968)
  Pallas kernels: 44.6 us -> 43.1 us
    pallas_call x1, Pallas kernels: 44.6 us -> 43.1 us  [narrow(): pl.pallas_call(functools.partial(step_body, bands, n_tile, n_grp), out_sh...]
where the time goes in v2:
time: 44.9 us; the launch traced here: 44.7 us
  Pallas kernels  43.1 us (96%)
  local copies, waits for them, and re-layouts  1.67 us (4%)
    pallas_call x1, Pallas kernels, narrow(): pl.pallas_call(functools.partial(step_body, bands, n_tile, n_grp), out_sh...  43.1 us
    unnamed x1, local copies, waits for them, and re-layouts  1.67 us

profile of v2, /device:TPU:0, one launch (start us, length us, event | category | flops | bytes accessed | tf_op | source)
XLA Modules:
  0.0 44.7 jit_solution(12772487639435748013)
XLA Ops:
  0.0 43.1 %shard_map.37 = bf16[256,512]{1,0:T(8,128)(2,1)} custom-call(s32[1,256]{1,0:T(1,128)} %bitcast.5, bf16[432,256]{1,0:T(8,128)(2,1)} %bitcast.3, bf16[432,128]{1,0:T(8,128)(2,1)} %bitcast.4), custom_call_target="tpu_custom_call" | custom-call | tf_op jit(solution)/shard_map/pallas_call | solution.py:469
  43.1 1.7 %copy.5 = bf16[256,512]{1,0:T(8,128)(2,1)} copy(bf16[256,512]{1,0:T(8,128)(2,1)} %shard_map.37) | data formatting | bytes 524288

commit v3 on v2

--- a/solution.py
+++ b/solution.py
@@ -198,9 +198,9 @@
 
 def step_body(
     bands, n_tile, n_grp,
-    lab_ref, pix_ref, tgt_ref, out_ref,
-    outgoing, arrived, counts, heard, library, outbound, returned, take_ref,
-    send_n, recv_n, send_a, recv_a, send_t, recv_t, send_b, recv_b,
+    lab_in, pix_in, tgt_in, out_ref,
+    lab_ref, pix_ref, tgt_ref, outgoing, arrived, counts, heard, library, outbound, returned, take_ref,
+    load_sem, send_n, recv_n, send_a, recv_a, send_t, recv_t, send_b, recv_b,
 ):
     devices = n_tile * n_grp
     full, rest = bands // LANES, bands % LANES
@@ -227,6 +227,14 @@
     for r in range(devices - 1, 0, -1):
         pl.semaphore_signal(barrier, inc=1, device_id=place(r), device_id_type=MESH)
 
+    pulls = [
+        pltpu.make_async_copy(src, dst, load_sem.at[i])
+        for i, (src, dst) in enumerate(((lab_in, lab_ref), (pix_in, pix_ref), (tgt_in, tgt_ref)))
+    ]
+    for cp in pulls:
+        cp.start()
+    for cp in pulls:
+        cp.wait()
     take, put, tally = slot_of(lab_ref[...], me, devices)
     take_ref[...] = take
     counts[...] = tally.reshape(devices, 1, LANES)
@@ -273,13 +281,13 @@
     across = flip(grp, 2)
     lends = [lend(0, tgt_ref, grp, 1), lend(1, tgt_ref, grp, 2), lend(2, library.at[across], across, 1)]
     half = devices // 2
-    late = devices - span
     for r in range(devices - 1, 0, -1):
         tell(r).start()
-    for r in range(1, half):
-        go(r).start()
-    for r in range(half, late):
-        go(r).start()
+    for i in range(half):
+        go(half + i).start()
+        for r in (4 * i + 1, 4 * i + 2, 4 * i + 3, 4 * i + 4):
+            if r < half:
+                go(r).start()
     lends[0].start()
     lends[1].start()
 
@@ -388,8 +396,6 @@
         tell(r).wait_recv()
     heads = jnp.maximum(jnp.sum(heard[...], axis=0), 1.0)
     number = [heads[:, c * STEP : c * STEP + 1] for c in range(OWNED)]
-    for r in range(late, devices):
-        go(r).start()
     for b in range(blocks):
         pair, maps = state.reduce(scale(b, rows))
         if b < blocks - 1:
@@ -443,10 +449,11 @@
             pieces.append(e * e * gain * lib[:, i : i + LANES])
         res.append(jnp.concatenate(pieces, axis=1).reshape(devices, 1, CAP, total))
     joined = jnp.concatenate(res, axis=1).reshape(devices, OWNED * CAP, total).astype(BF16)
-    for lo, hi in ((half, devices), (0, half)):
-        outbound[lo:hi] = joined[lo:hi]
-        for r in range(hi - 1, max(lo, 1) - 1, -1):
-            back(r).start()
+    outbound[...] = joined
+    for i in range(half):
+        back(half + i).start()
+        if i:
+            back(i).start()
     returned[0] = outbound[0]
     for r in range(1, devices):
         tell(r).wait_send()
@@ -469,9 +476,12 @@
     return pl.pallas_call(
         functools.partial(step_body, bands, n_tile, n_grp),
         out_shape=jax.ShapeDtypeStruct((rows, total), BF16),
-        in_specs=[vmem] * 3,
+        in_specs=[pl.BlockSpec(memory_space=pl.ANY)] * 3,
         out_specs=vmem,
         scratch_shapes=[
+            pltpu.VMEM((1, rows), labels.dtype),
+            pltpu.VMEM((bands, rows), BF16),
+            pltpu.VMEM((bands, targets.shape[0]), BF16),
             pltpu.VMEM((devices, deep, LANES), BF16),
             pltpu.VMEM((devices, deep, LANES), BF16),
             pltpu.VMEM((devices, 1, LANES), F32),
@@ -480,6 +490,7 @@
             pltpu.VMEM((devices, OWNED * CAP, total), BF16),
             pltpu.VMEM((devices, OWNED * CAP, total), BF16),
             pltpu.VMEM((rows, NCLUST * CAP), BF16),
+            dma((3,)),
             dma((devices,)), dma((devices,)),
             dma((devices,)), dma((devices,)),
             dma((n_grp,)), dma((n_grp,)),

time: 44.9 us -> 42.4 us (0.944)
  Pallas kernels: 43.1 us -> 40.3 us
    pallas_call x1, Pallas kernels: 43.1 us -> 40.3 us  [narrow(): pl.pallas_call(functools.partial(step_body, bands, n_tile, n_grp), out_sh...]
where the time goes in v3:
time: 42.4 us; the launch traced here: 42 us
  Pallas kernels  40.3 us (95%)
  local copies, waits for them, and re-layouts  1.67 us (4%)
    pallas_call x1, Pallas kernels, narrow(): pl.pallas_call(functools.partial(step_body, bands, n_tile, n_grp), out_sh...  40.3 us
    unnamed x1, local copies, waits for them, and re-layouts  1.67 us

profile of v3, /device:TPU:0, one launch (start us, length us, event | category | flops | bytes accessed | tf_op | source)
XLA Modules:
  0.0 42.0 jit_solution(9779681115129569716)
XLA Ops:
  0.0 40.3 %shard_map.37 = bf16[256,512]{1,0:T(8,128)(2,1)} custom-call(s32[1,256]{1,0:T(1,128)} %bitcast.5, bf16[432,256]{1,0:T(8,128)(2,1)} %bitcast.3, bf16[432,128]{1,0:T(8,128)(2,1)} %bitcast.4), custom_call_target="tpu_custom_call" | custom-call | tf_op jit(solution)/shard_map/pallas_call | solution.py:476
  40.3 1.7 %copy.5 = bf16[256,512]{1,0:T(8,128)(2,1)} copy(bf16[256,512]{1,0:T(8,128)(2,1)} %shard_map.37) | data formatting | bytes 524288

commit v4 on v3

--- a/solution.py
+++ b/solution.py
@@ -284,12 +284,13 @@
     for r in range(devices - 1, 0, -1):
         tell(r).start()
     for i in range(half):
-        go(half + i).start()
-        for r in (4 * i + 1, 4 * i + 2, 4 * i + 3, 4 * i + 4):
+        for r in range(7 * i + 1, 7 * i + 8):
             if r < half:
                 go(r).start()
-    lends[0].start()
-    lends[1].start()
+        go(half + i).start()
+        if i == 3:
+            lends[0].start()
+            lends[1].start()
 
     lane = lax.broadcasted_iota(jnp.int32, (STEP, LANES), 1)
     own = [((lane >= c * rest) & (lane < (c + 1) * rest)) for c in range(OWNED)]
@@ -396,13 +397,16 @@
         tell(r).wait_recv()
     heads = jnp.maximum(jnp.sum(heard[...], axis=0), 1.0)
     number = [heads[:, c * STEP : c * STEP + 1] for c in range(OWNED)]
+    def prefetch(b):
+        held["rows"] = gram(b, fetch(b))
+
     for b in range(blocks):
         pair, maps = state.reduce(scale(b, rows))
         if b < blocks - 1:
-            factor = paired_factor(pair, [])
+            hold = [lambda: None] * 11
+            factor = paired_factor(pair, hold + [functools.partial(prefetch, b + 1)])
             state.extend(factor, maps)
-            lean = fetch(b + 1)
-            rows = gram(b + 1, lean)
+            rows = held["rows"]
             if not b:
                 lends[1].wait_recv()
                 lends[2].start()

time: 42.4 us -> 42.1 us (level)
  no operation moved by 1% of the time
where the time goes in v4:
time: 42.1 us; the launch traced here: 41.9 us
  Pallas kernels  40.2 us (95%)
  local copies, waits for them, and re-layouts  1.67 us (4%)
    pallas_call x1, Pallas kernels, narrow(): pl.pallas_call(functools.partial(step_body, bands, n_tile, n_grp), out_sh...  40.2 us
    unnamed x1, local copies, waits for them, and re-layouts  1.67 us

profile of v4, /device:TPU:0, one launch (start us, length us, event | category | flops | bytes accessed | tf_op | source)
XLA Modules:
  0.0 41.9 jit_solution(9534321480129655584)
XLA Ops:
  0.0 40.2 %shard_map.37 = bf16[256,512]{1,0:T(8,128)(2,1)} custom-call(s32[1,256]{1,0:T(1,128)} %bitcast.5, bf16[432,256]{1,0:T(8,128)(2,1)} %bitcast.3, bf16[432,128]{1,0:T(8,128)(2,1)} %bitcast.4), custom_call_target="tpu_custom_call" | custom-call | tf_op jit(solution)/shard_map/pallas_call | solution.py:480
  40.2 1.7 %copy.5 = bf16[256,512]{1,0:T(8,128)(2,1)} copy(bf16[256,512]{1,0:T(8,128)(2,1)} %shard_map.37) | data formatting | bytes 524288
